TPU v7x, 32 devices: a whole 2x2x4 slice. The times are simulated.
32 devices in a mesh: groups: 2 (over x), utt: 16 (over z, y, core).
Axes of the slice: x: 2, y: 2, z: 4, core: 2. Of those that a mesh axis runs over, the one named last changes fastest.
Arguments:
- waveforms: float32 [64, 90], P(('groups', 'utt')), parts along dimension 0, may hold values from -6 to 6
- lengths: int32 [64], P(('groups', 'utt')), parts along dimension 0, may hold values from 1 to 7, as said below
- take_list: int32 [64], P(('groups', 'utt')), parts along dimension 0, may hold values from 0 to 31, as said below
- conv_first: float32 [3, 10, 512], replicated, may hold values from -2 to 2
- conv_second: bfloat16 [3, 1536, 512], replicated, may hold values from -0.15625 to 0.15625
- norm_gain: float32 [3, 2, 512], replicated, may hold values from 0.5 to 1.5
- norm_shift: float32 [3, 2, 512], replicated, may hold values from -2 to 2
- enc_weight: bfloat16 [1536, 8192], P(None, 'utt'), may hold values from -0.15625 to 0.15625
- enc_bias: float32 [8192], P('utt'), may hold values from -2 to 2
- dec_weight: bfloat16 [8192, 1536], P('utt'), may hold values from -0.0625 to 0.0625
- dec_bias: float32 [1536], replicated, may hold values from -2 to 2
Outputs:
- enc_grad: bfloat16 [3072, 8192], P('groups', 'utt'), parts along dimension 0
- dec_grad: bfloat16 [16384, 1536], P(('groups', 'utt')), parts along dimension 0
- enc_bias_grad: float32 [16384], P(('groups', 'utt')), parts along dimension 0
- dec_bias_grad: float32 [3072], P('groups'), parts along dimension 0
- mean_loss: float32 [2], P('groups'), parts along dimension 0
- errors_out: bfloat16 [256, 1536], P(('groups', 'utt')), parts along dimension 0
There are 2 independent parts, one for each index of `groups`. A program takes and returns all parts, laid end to end along the dimension named above; an argument that names none is the same for every part. Nothing has to cross between parts.
Inputs may be any that keep to these rules, and one draw needn't show every extreme that they name: Valid frames of each utterance; the 32 lengths sum to 128, and some utterance has exactly 7. `take_list`: a permutation of the utterances: entry d * 2 + k names the utterance that slot k of device d takes; the utterances taken by the slots of one device have 8 valid frames together.
All inputs are finite; a program needn't handle non-finite values.
Results may differ from a plain program's by a relative error of at most 0.0095.
Values may be sent and summed in bfloat16 or wider, within the bound.
No kernel may reach another device: no remote copies, remote signals or barrier semaphores. Data moves between devices by JAX's collectives and lax.ppermute only.
A program may use at most 128 MiB of HBM per device.

v0:
```python
import jax
import jax.numpy as jnp
from jax import lax
from jax.sharding import PartitionSpec as P

ROWS_DEV = 8
sparsity = 0.5
epsilon = 1e-05


def normalize(values, gain, shift):
    center = values - jnp.mean(values, axis=-1, keepdims=True)
    spread = jnp.mean(center * center, axis=-1, keepdims=True)
    return center * lax.rsqrt(spread + epsilon) * gain + shift


def extract(chosen, conv_first, conv_second, norm_gain, norm_shift):
    count = chosen.shape[0]
    frames = (chosen.shape[1] - 10) // 10
    checkpoints = conv_first.shape[0]
    channels = conv_first.shape[2]
    blocks = chosen.reshape(count, 2 * frames + 2, 5)
    windows = jnp.concatenate([blocks[:, :-1], blocks[:, 1:]], axis=-1)
    first = jnp.einsum("ntk,ckd->cntd", windows, conv_first, precision=lax.Precision.HIGHEST)
    first = normalize(first, norm_gain[:, 0][:, None, None, :], norm_shift[:, 0][:, None, None, :])
    first = jax.nn.gelu(first, approximate=False).astype(jnp.bfloat16)
    paired = first[:, :, :-1].reshape(checkpoints, count, frames, 2 * channels)
    columns = jnp.concatenate([paired, first[:, :, 2::2]], axis=-1)
    second = jnp.einsum("cntk,ckd->cntd", columns, conv_second, preferred_element_type=jnp.float32)
    second = normalize(
        second, norm_gain[:, 1][:, None, None, :], norm_shift[:, 1][:, None, None, :]
    )
    second = jax.nn.gelu(second, approximate=False).astype(jnp.bfloat16)
    return second.transpose(1, 2, 0, 3).reshape(count, frames, checkpoints * channels)


def shards(
    waveforms,
    lengths,
    take_list,
    conv_first,
    conv_second,
    norm_gain,
    norm_shift,
    enc_weight,
    enc_bias,
    dec_weight,
    dec_bias,
):
    slots = take_list.shape[0]
    devices = lax.axis_size("utt")
    tokens = ROWS_DEV * devices
    position = lax.axis_index("utt")
    piece_sound = lax.all_gather(waveforms, "utt", axis=0, tiled=True)
    piece_length = lax.all_gather(lengths, "utt", axis=0, tiled=True)
    labels = jnp.arange(piece_sound.shape[0], dtype=jnp.int32)
    match = take_list[:, None] == labels[None, :]
    sound_sum = jnp.dot(match.astype(jnp.float32), piece_sound, precision=lax.Precision.HIGHEST)
    length_sum = jnp.sum(jnp.where(match, piece_length[None, :], 0), axis=1).astype(jnp.int32)
    frames = extract(sound_sum, conv_first, conv_second, norm_gain, norm_shift)
    frame_count = frames.shape[1]
    feature = frames.shape[2]
    flat_frames = frames.reshape(slots * frame_count, feature)
    local_start = jnp.cumsum(length_sum) - length_sum
    frame_index = jnp.arange(frame_count, dtype=jnp.int32)
    valid = frame_index[None, :] < length_sum[:, None]
    before = position * ROWS_DEV
    targets = jnp.where(valid, before + local_start[:, None] + frame_index[None, :], tokens)
    targets = targets.reshape(-1)
    all_frames, all_targets = (
        lax.all_gather(flat_frames, "utt", axis=0, tiled=True),
        lax.all_gather(targets, "utt", axis=0, tiled=True),
    )
    inputs = jnp.zeros((tokens + 1, feature), jnp.bfloat16).at[all_targets].set(all_frames)[:tokens]
    latents_dev = enc_weight.shape[1]
    checkpoints = conv_first.shape[0]
    channels = conv_first.shape[2]
    preact = jnp.dot(inputs, enc_weight, preferred_element_type=jnp.float32) + enc_bias
    latent = jnp.maximum(preact, 0.0)
    latent_b = latent.astype(jnp.bfloat16)
    decoder = dec_weight.astype(jnp.float32).reshape(latents_dev, checkpoints, channels)
    norms = jnp.sqrt(jnp.sum(decoder * decoder, axis=-1) + 1e-06)
    weights_sum = jnp.sum(norms, axis=-1)
    partial_recon = jnp.dot(latent_b, dec_weight, preferred_element_type=jnp.float32)
    recon = lax.psum(partial_recon, "utt")
    errors = recon + dec_bias - inputs.astype(jnp.float32)
    errors_b = errors.astype(jnp.bfloat16)
    own_errors = lax.dynamic_slice_in_dim(errors, position * ROWS_DEV, ROWS_DEV, 0)
    loss_part = jnp.sum(own_errors * own_errors) + sparsity * jnp.sum(latent * weights_sum)
    bias_part = jnp.sum(2.0 * own_errors, axis=0)
    dec_bias_grad, loss_total = lax.psum((bias_part, loss_part), "utt")
    mean_loss = (loss_total / (tokens * feature)).reshape(1)
    activity = jnp.sum(latent, axis=0)
    dec_grad = 2.0 * jnp.dot(latent_b.T, errors_b, preferred_element_type=jnp.float32)
    dec_grad = dec_grad + sparsity * (
        activity[:, None, None] * decoder / norms[:, :, None]
    ).reshape(latents_dev, feature)
    upstream = (
        2.0 * jnp.dot(errors_b, dec_weight.T, preferred_element_type=jnp.float32)
        + sparsity * weights_sum
    )
    through = jnp.where(preact > 0.0, upstream, 0.0)
    enc_grad = jnp.dot(inputs.T, through.astype(jnp.bfloat16), preferred_element_type=jnp.float32)
    return (
        enc_grad.astype(jnp.bfloat16),
        dec_grad.astype(jnp.bfloat16),
        jnp.sum(through, axis=0),
        dec_bias_grad,
        mean_loss,
        own_errors.astype(jnp.bfloat16),
    )


def solution(mesh):
    return jax.shard_map(
        shards,
        mesh=mesh,
        in_specs=(
            P(("groups", "utt"), None),
            P(("groups", "utt")),
            P(("groups", "utt")),
            P(),
            P(),
            P(),
            P(),
            P(None, "utt"),
            P("utt"),
            P("utt", None),
            P(),
        ),
        out_specs=(
            P("groups", "utt"),
            P(("groups", "utt"), None),
            P(("groups", "utt")),
            P("groups"),
            P("groups"),
            P(("groups", "utt"), None),
        ),
        check_vma=False,
    )
```

profile of v0, /device:TPU:0, one launch (start us, length us, event | category | flops | bytes accessed | tf_op | source)
XLA Modules:
  0.0 240.3 jit_solution(2240350737570929996)
XLA Ops:
  7.2 23.5 %all-gather = f32[16,2,90]{2,1,0:T(2,128)S(1)} all-gather(f32[1,2,90]{2,1,0:T(2,128)} %bitcast.74), channel_id=1, replica_groups=mesh['groups'=2,'utt'=16] {'utt'}, dimensions={0}, use_global_device_ids=true | all-gather | bytes 12240 | tf_op jit(solution)/shard_map/all_gather | solution.py:54
  30.7 0.8 fusion.44
  31.8 1.4 fusion.55
  33.3 0.2 multiply_reduce_fusion
  33.5 0.8 fusion.54
  34.3 0.8 fusion.53
  35.1 0.8 fusion.12
  36.1 3.3 %fusion.56 = (f32[3,2,8]{2,1,0:T(2,128)S(1)}, f32[3,2,8,512]{3,2,1,0:T(8,128)S(1)}) fusion(bf16[3,1536,512]{2,1,0:T(8,128)(2,1)} %param.15, bf16[3,2,8,512]{3,2,0,1:T(8,128)(2,1)S(1)} %slice.32, bf16[3,2,8,1024]{3,2,0,1:T(8,128)(2,1)S(1)} %reshape.107), kind=kOutput, calls=%fused_computation.111 | convolution fusion | flops 75816912 | bytes 4964544 | tf_op jit(solution)/shard_map/cntk,ckd->cntd/dot_general | solution.py:29
  39.6 0.3 fusion.28
  40.0 21.0 %all_gather.15 = bf16[256,1536]{1,0:T(8,128)(2,1)} all-gather(bf16[16,1536]{1,0:T(8,128)(2,1)S(1)} %bitcast.71), channel_id=1, replica_groups=mesh['groups'=2,'utt'=16] {'utt'}, dimensions={0}, use_global_device_ids=true | all-gather | bytes 835584 | tf_op jit(solution)/shard_map/all_gather | solution.py:71
  61.0 0.6 dynamic-slice
  62.2 0.2 dynamic-update-slice
  62.5 9.6 %all-reduce = s32[32]{0:T(128)S(1)} all-reduce(s32[32]{0:T(128)S(1)} %dynamic-update-slice), channel_id=1, replica_groups=mesh['groups'=2,'utt'=16] {'utt'}, use_global_device_ids=true, to_apply=%add | all-reduce | flops 32 | bytes 256
  72.1 0.2 select_reduce_fusion
  73.3 0.2 dynamic-update-slice.1
  73.5 11.2 %all-reduce.1 = s32[256]{0:T(256)S(1)} all-reduce(s32[256]{0:T(256)S(1)} %dynamic-update-slice.1), channel_id=1, replica_groups=mesh['groups'=2,'utt'=16] {'utt'}, use_global_device_ids=true, to_apply=%add.1 | all-reduce | flops 256 | bytes 2048
  84.8 2.1 convert_multiply_fusion.1
  86.9 3.6 %copy.44 = f32[512,1536]{0,1:T(8,128)} copy(f32[512,1536]{1,0:T(8,128)} %convert_multiply_fusion.1) | data formatting | bytes 6291456 | tf_op jit(solution)/shard_map/mul | solution.py:82
  90.5 2.1 reduce_sum.113
  92.6 3.1 %scatter_custom_fusion = bf16[129,1536]{1,0:T(8,128)(2,1)} fusion(s32[256]{0:T(256)S(1)} %compare_select_fusion, bf16[256,1536]{1,0:T(8,128)(2,1)} %all_gather.15, bf16[]{:T(256)} %constant.40.clone.1), kind=kCustom, calls=%fused_computation.43 | custom fusion | bytes 396800 | tf_op jit(solution)/shard_map/scatter | solution.py:74
  95.7 2.0 multiply_reduce_fusion.1
  97.7 1.3 fusion.41
  99.0 2.1 div.33
  101.1 3.6 %copy.45 = f32[512,1536]{1,0:T(8,128)} copy(f32[512,1536]{0,1:T(8,128)} %bitcast.70) | data formatting | bytes 6291456 | tf_op jit(solution)/shard_map/div | solution.py:96
  105.4 83.7 %all-reduce.5.cloned.1.call-done = f32[128,1536]{1,0:T(8,128)} async-done(((f32[128,1536]{1,0:T(8,128)}), f32[128,1536]{1,0:T(8,128)}) %all-reduce.5.cloned.1.call-update) | async-done | bytes 786448 | tf_op jit(solution)/shard_map/psum | solution.py:85
  189.1 1.4 convert_subtract_fusion
  190.5 0.7 multiply_reduce_fusion.3
  191.3 0.6 dynamic-slice_convert_fusion
  191.9 1.3 fusion.57
  193.1 1.7 convolution_convert_fusion
  195.5 31.9 %all-reduce.2 = (f32[1536]{0:T(1024)}, f32[]{:T(128)}) all-reduce(f32[1536]{0:T(1024)S(1)} %get-tuple-element.7, f32[]{:T(128)S(6)} %add.150), channel_id=1, replica_groups=mesh['groups'=2,'utt'=16] {'utt'}, use_global_device_ids=true, to_apply=%region_13.14 | all-reduce | flops 1537 | bytes 12296 | tf_op jit(solution)/shard_map/psum | solution.py:91
  228.1 4.2 %fusion.5 = bf16[512,1536]{1,0:T(8,128)(2,1)} fusion(f32[512,1536]{1,0:T(8,128)} %copy.45, bf16[512,1536]{1,0:T(8,128)(2,1)S(1)} %copy-done.1, f32[512]{0:T(512)S(1)} %get-tuple-element.9, f32[128,1536]{1,0:T(8,128)} %copy-done.3, f32[128,512]{1,0:T(8,128)S(1)} %get-tuple-element.26), kind=kOutput, calls=%fused_computation.9 | convolution fusion | flops 207159296 | bytes 7342080 | tf_op jit(solution)/shard_map/dot_general | solution.py:94
  (45 shorter events, 1.2 us)
Async XLA Ops:
  7.2 88.5 %copy-start = (bf16[1536,512]{1,0:T(8,128)(2,1)S(1)}, bf16[1536,512]{1,0:T(8,128)(2,1)}, u32[]{:S(2)}) copy-start(bf16[1536,512]{1,0:T(8,128)(2,1)} %param.18) | copy-start | bytes 4718596
  7.2 181.9 %all-reduce.5.cloned.1.call-start = ((), (), s32[]{:S(2)}) async-start(), calls=%async_computation | async-start | bytes 1572864 | tf_op jit(solution)/shard_map/psum | solution.py:85
  36.1 24.9 %copy-start.8 = (u32[32]{0:T(128)S(1)}, u32[32]{0:T(128)}, u32[]{:S(2)}) copy-start(u32[32]{0:T(128)} %constant.13) | copy-start | bytes 388
  36.1 26.1 %copy-start.6 = (s32[2]{0:T(128)S(1)}, s32[2]{0:T(128)}, u32[]{:S(2)}) copy-start(s32[2]{0:T(128)} %param.12) | copy-start | bytes 28
  36.1 36.0 %copy-start.7 = (s32[2]{0:T(128)S(1)}, s32[2]{0:T(128)}, u32[]{:S(2)}) copy-start(s32[2]{0:T(128)} %param.13) | copy-start | bytes 28
  36.1 48.7 %copy-start.1 = (bf16[512,1536]{1,0:T(8,128)(2,1)S(1)}, bf16[512,1536]{1,0:T(8,128)(2,1)}, u32[]{:S(2)}) copy-start(bf16[512,1536]{1,0:T(8,128)(2,1)} %param.20) | copy-start | bytes 4718596
  90.5 5.3 %copy-start.5 = (f32[512]{0:T(512)S(1)}, f32[512]{0:T(512)}, u32[]{:S(2)}) copy-start(f32[512]{0:T(512)} %param.19) | copy-start | bytes 6148
  101.1 88.0 %copy-start.4 = (f32[1536]{0:T(1024)S(1)}, f32[1536]{0:T(1024)}, u32[]{:S(2)}) copy-start(f32[1536]{0:T(1024)} %param.21) | copy-start | bytes 18436
  189.1 4.0 %copy-start.2 = (bf16[129,1536]{1,0:T(8,128)(2,1)S(1)}, bf16[129,1536]{1,0:T(8,128)(2,1)}, u32[]{:S(2)}) copy-start(bf16[129,1536]{1,0:T(8,128)(2,1)} %scatter_custom_fusion) | copy-start | bytes 1188868
  190.5 4.4 %copy-start.3 = (f32[128,1536]{1,0:T(8,128)}, f32[128,1536]{1,0:T(8,128)S(1)}, u32[]{:S(2)}) copy-start(f32[128,1536]{1,0:T(8,128)S(1)} %convert_subtract_fusion) | copy-start | bytes 2359300
Sparse Core Ops, SparseCore 0:
  99.1 89.9 all-reduce.4
where the time goes:
time: 241 us; the launch traced here: 240 us
  blocking collectives  97.2 us (40%)
  waiting for transfers between devices  83.8 us (35%)
  between operations  18.7 us (8%)
  local copies, waits for them, and re-layouts  16.3 us (7%)
  matrix products  16 us (7%)
  other arithmetic  8.29 us (3%)
    psum x1, waiting for transfers between devices, shards(): recon = lax.psum(partial_recon, 'utt')  83.7 us
    psum x1, blocking collectives, shards(): dec_bias_grad, loss_total = lax.psum((bias_part, loss_part), 'utt')  31.9 us
    all_gather x1, blocking collectives, shards(): piece_sound = lax.all_gather(waveforms, 'utt', axis=0, tiled=True)  23.5 us
    all_gather x1, blocking collectives, shards(): lax.all_gather(flat_frames, 'utt', axis=0, tiled=True)  21 us
    unnamed x2, blocking collectives  20.8 us
    div x2, local copies, waits for them, and re-layouts, shards(): activity[:, None, None] * decoder / norms[:, :, None]  5.7 us
  transfers between devices with their start and end apart: 1, of which 1 were waited for; matrix products, arithmetic and copies ran while one was open for 2% of the time, Pallas kernels for 0%

commit v1 on v0

--- a/solution.py
+++ b/solution.py
@@ -82,7 +82,7 @@
     norms = jnp.sqrt(jnp.sum(decoder * decoder, axis=-1) + 1e-06)
     weights_sum = jnp.sum(norms, axis=-1)
     partial_recon = jnp.dot(latent_b, dec_weight, preferred_element_type=jnp.float32)
-    recon = lax.psum(partial_recon, "utt")
+    recon = jnp.sum(lax.all_gather(partial_recon, "utt"), axis=0)
     errors = recon + dec_bias - inputs.astype(jnp.float32)
     errors_b = errors.astype(jnp.bfloat16)
     own_errors = lax.dynamic_slice_in_dim(errors, position * ROWS_DEV, ROWS_DEV, 0)

time: 241 us -> 258 us (1.071)
  waiting for transfers between devices: 83.8 us -> 92.5 us
  other arithmetic: 8.29 us -> 15.7 us
    all_gather x0 -> x1, waiting for transfers between devices: none -> 92.5 us  [shards(): recon = jnp.sum(lax.all_gather(partial_recon, 'utt'), axis=0)]
    psum x1 -> x0, waiting for transfers between devices: 83.7 us -> none  [shards(): recon = lax.psum(partial_recon, 'utt')]
    reduce_sum x0 -> x1, other arithmetic: none -> 6.76 us  [shards(): recon = jnp.sum(lax.all_gather(partial_recon, 'utt'), axis=0)]
where the time goes in v1:
time: 258 us
  blocking collectives  97.4 us (38%)
  waiting for transfers between devices  92.5 us (36%)
  between operations  18.6 us (7%)
  local copies, waits for them, and re-layouts  17.5 us (7%)
  matrix products  16 us (6%)
  other arithmetic  15.7 us (6%)
    all_gather x1, waiting for transfers between devices, shards(): recon = jnp.sum(lax.all_gather(partial_recon, 'utt'), axis=0)  92.5 us
    psum x1, blocking collectives, shards(): dec_bias_grad, loss_total = lax.psum((bias_part, loss_part), 'utt')  32.3 us
    all_gather x1, blocking collectives, shards(): piece_sound = lax.all_gather(waveforms, 'utt', axis=0, tiled=True)  23.4 us
    all_gather x1, blocking collectives, shards(): lax.all_gather(flat_frames, 'utt', axis=0, tiled=True)  21.5 us
    unnamed x2, blocking collectives  20.2 us
    reduce_sum x1, other arithmetic, shards(): recon = jnp.sum(lax.all_gather(partial_recon, 'utt'), axis=0)  6.76 us
    div x2, local copies, waits for them, and re-layouts, shards(): activity[:, None, None] * decoder / norms[:, :, None]  5.61 us
  transfers between devices with their start and end apart: 1, of which 1 were waited for; matrix products, arithmetic and copies ran while one was open for 2% of the time, Pallas kernels for 0%

profile of v1, /device:TPU:0, one launch (start us, length us, event | category | flops | bytes accessed | tf_op | source)
XLA Modules:
  0.0 257.7 jit_solution(2869941331871506544)
XLA Ops:
  7.2 0.8 fusion.53
  8.1 0.8 fusion.54
  8.9 23.4 %all-gather.1 = f32[16,2,90]{2,1,0:T(2,128)S(1)} all-gather(f32[1,2,90]{2,1,0:T(2,128)} %bitcast.77), channel_id=1, replica_groups=mesh['groups'=2,'utt'=16] {'utt'}, dimensions={0}, use_global_device_ids=true | all-gather | bytes 12240 | tf_op jit(solution)/shard_map/all_gather | solution.py:54
  32.2 0.8 fusion.44
  33.4 1.4 fusion.55
  35.0 0.8 fusion.12
  36.0 1.2 dynamic-slice
  38.5 0.9 dynamic-update-slice
  39.4 7.1 %all-reduce = s32[32]{0:T(128)S(1)} all-reduce(s32[32]{0:T(128)S(1)} %dynamic-update-slice), channel_id=1, replica_groups=mesh['groups'=2,'utt'=16] {'utt'}, use_global_device_ids=true, to_apply=%add | all-reduce | flops 32 | bytes 256
  46.5 0.8 select_reduce_fusion
  47.7 0.2 dynamic-update-slice.1
  47.9 13.0 %all-reduce.1 = s32[256]{0:T(256)S(1)} all-reduce(s32[256]{0:T(256)S(1)} %dynamic-update-slice.1), channel_id=1, replica_groups=mesh['groups'=2,'utt'=16] {'utt'}, use_global_device_ids=true, to_apply=%add.1 | all-reduce | flops 256 | bytes 2048
  61.0 3.3 %fusion.56 = (f32[3,2,8]{2,1,0:T(2,128)S(1)}, f32[3,2,8,512]{3,2,1,0:T(8,128)S(1)}) fusion(bf16[3,1536,512]{2,1,0:T(8,128)(2,1)} %param.15, bf16[3,2,8,512]{3,2,0,1:T(8,128)(2,1)S(1)} %slice.32, bf16[3,2,8,1024]{3,2,0,1:T(8,128)(2,1)S(1)} %reshape.107), kind=kOutput, calls=%fused_computation.111 | convolution fusion | flops 75816912 | bytes 4964544 | tf_op jit(solution)/shard_map/cntk,ckd->cntd/dot_general | solution.py:29
  64.4 0.3 fusion.28
  64.8 21.5 %all_gather.21 = bf16[256,1536]{1,0:T(8,128)(2,1)} all-gather(bf16[16,1536]{1,0:T(8,128)(2,1)S(1)} %bitcast.74), channel_id=1, replica_groups=mesh['groups'=2,'utt'=16] {'utt'}, dimensions={0}, use_global_device_ids=true | all-gather | bytes 835584 | tf_op jit(solution)/shard_map/all_gather | solution.py:71
  86.4 2.1 convert_multiply_fusion.1
  88.5 3.6 %copy.44 = f32[512,1536]{0,1:T(8,128)} copy(f32[512,1536]{1,0:T(8,128)} %convert_multiply_fusion.1) | data formatting | bytes 6291456 | tf_op jit(solution)/shard_map/mul | solution.py:82
  92.0 2.1 reduce_sum.123
  94.2 3.1 %scatter_custom_fusion = bf16[129,1536]{1,0:T(8,128)(2,1)} fusion(s32[256]{0:T(256)S(1)} %compare_select_fusion, bf16[256,1536]{1,0:T(8,128)(2,1)} %all_gather.21, bf16[]{:T(256)} %constant.40.clone.1), kind=kCustom, calls=%fused_computation.43 | custom fusion | bytes 396800 | tf_op jit(solution)/shard_map/scatter | solution.py:74
  97.3 2.0 multiply_reduce_fusion.1
  99.3 1.3 fusion.41
  100.6 2.1 div.33
  102.7 3.6 %copy.45 = f32[512,1536]{1,0:T(8,128)} copy(f32[512,1536]{0,1:T(8,128)} %bitcast.72) | data formatting | bytes 6291456 | tf_op jit(solution)/shard_map/div | solution.py:96
  106.9 92.5 %all-gather.4.cloned.1.call-done = f32[2048,1536]{1,0:T(8,128)} async-done(((f32[128,1536]{1,0:T(8,128)}), f32[2048,1536]{1,0:T(8,128)}) %all-gather.4.cloned.1.call-update) | async-done | bytes 12582928 | tf_op jit(solution)/shard_map/all_gather | solution.py:85
  199.4 6.8 %reduce_sum.122 = f32[128,1536]{1,0:T(8,128)} reduce(f32[16,128,1536]{2,1,0:T(8,128)} %bitcast.73, f32[]{:T(128)} %constant.46.clone.1), dimensions={0}, to_apply=%region_7.8 | reduce | flops 2949120 | bytes 13369348 | tf_op jit(solution)/shard_map/reduce_sum | solution.py:85
  206.1 1.4 convert_subtract_fusion
  207.5 0.7 multiply_reduce_fusion.3
  208.3 0.6 dynamic-slice_convert_fusion
  208.9 1.3 fusion.57
  210.1 1.7 convolution_convert_fusion
  212.5 32.3 %all-reduce.2 = (f32[1536]{0:T(1024)}, f32[]{:T(128)}) all-reduce(f32[1536]{0:T(1024)S(1)} %get-tuple-element.7, f32[]{:T(128)S(6)} %add.148), channel_id=1, replica_groups=mesh['groups'=2,'utt'=16] {'utt'}, use_global_device_ids=true, to_apply=%region_13.14 | all-reduce | flops 1537 | bytes 12296 | tf_op jit(solution)/shard_map/psum | solution.py:91
  245.5 4.2 %fusion.5 = bf16[512,1536]{1,0:T(8,128)(2,1)} fusion(f32[512,1536]{1,0:T(8,128)} %copy.45, bf16[512,1536]{1,0:T(8,128)(2,1)S(1)} %copy-done.1, f32[512]{0:T(512)S(1)} %get-tuple-element.9, f32[128,1536]{1,0:T(8,128)} %copy-done.3, f32[128,512]{1,0:T(8,128)S(1)} %get-tuple-element.26), kind=kOutput, calls=%fused_computation.9 | convolution fusion | flops 207159296 | bytes 7342080 | tf_op jit(solution)/shard_map/dot_general | solution.py:94
  (40 shorter events, 1.4 us)
Async XLA Ops:
  7.2 90.1 %copy-start = (bf16[1536,512]{1,0:T(8,128)(2,1)S(1)}, bf16[1536,512]{1,0:T(8,128)(2,1)}, u32[]{:S(2)}) copy-start(bf16[1536,512]{1,0:T(8,128)(2,1)} %param.18) | copy-start | bytes 4718596
  7.2 192.2 %all-gather.4.cloned.1.call-start = ((), (), s32[]{:S(2)}) async-start(), calls=%async_computation | async-start | bytes 13369344 | tf_op jit(solution)/shard_map/all_gather | solution.py:85
  61.0 25.4 %copy-start.1 = (bf16[512,1536]{1,0:T(8,128)(2,1)S(1)}, bf16[512,1536]{1,0:T(8,128)(2,1)}, u32[]{:S(2)}) copy-start(bf16[512,1536]{1,0:T(8,128)(2,1)} %param.20) | copy-start | bytes 4718596
  92.0 5.3 %copy-start.5 = (f32[512]{0:T(512)S(1)}, f32[512]{0:T(512)}, u32[]{:S(2)}) copy-start(f32[512]{0:T(512)} %param.19) | copy-start | bytes 6148
  199.4 6.8 %copy-start.4 = (f32[1536]{0:T(1024)S(1)}, f32[1536]{0:T(1024)}, u32[]{:S(2)}) copy-start(f32[1536]{0:T(1024)} %param.21) | copy-start | bytes 18436
  206.1 4.0 %copy-start.2 = (bf16[129,1536]{1,0:T(8,128)(2,1)S(1)}, bf16[129,1536]{1,0:T(8,128)(2,1)}, u32[]{:S(2)}) copy-start(bf16[129,1536]{1,0:T(8,128)(2,1)} %scatter_custom_fusion) | copy-start | bytes 1188868
  207.5 4.3 %copy-start.3 = (f32[128,1536]{1,0:T(8,128)}, f32[128,1536]{1,0:T(8,128)S(1)}, u32[]{:S(2)}) copy-start(f32[128,1536]{1,0:T(8,128)S(1)} %convert_subtract_fusion) | copy-start | bytes 2359300
Sparse Core Ops, SparseCore 0:
  100.7 98.6 all-gather.3
